TPU v7x, 32 devices: a whole 2x2x4 slice. The times are simulated.
32 devices in a mesh: grp: 2 (over y), ctx: 4 (over z), sub: 4 (over x, core).
Axes of the slice: x: 2, y: 2, z: 4, core: 2. Of those that a mesh axis runs over, the one named last changes fastest.
Arguments:
- queries: bfloat16 [64, 3072], P(('grp', 'ctx'), 'sub'), parts along dimension 0, may hold values from -1024 to 1024
- latent_cache: bfloat16 [3072, 576], P(('grp', 'ctx')), parts along dimension 0, may hold values from -8 to 8
- cache_len: int32 [8], P(('grp', 'ctx')), parts along dimension 0, may hold values from 16 to 384, as said below
- kv_up: bfloat16 [32, 256, 512], P(('grp', 'sub'), None, 'ctx'), parts along dimension 0, may hold values from -1 to 1
- o_weight: bfloat16 [2048, 2048], P('sub', 'ctx'), may hold values from -0.5 to 0.5
- residual: bfloat16 [64, 2048], P(('grp', 'ctx')), parts along dimension 0, may hold values from -3 to 3
- norm_gain: bfloat16 [2048], replicated, may hold values from 0.25 to 1.75
- route_ids: int32 [64, 6], P(('grp', 'ctx')), parts along dimension 0, may hold values from 0 to 63, all different within a row; in each aligned block of 8 rows (0 to 7, 8 to 15, ...) at most 2 rows name the same one
- route_weights: float32 [64, 6], P(('grp', 'ctx')), parts along dimension 0, may hold values from 0.1 to 0.6
- w_gate: bfloat16 [64, 2048, 1408], P('ctx', None, 'sub'), may hold values from -0.125 to 0.125
- w_up: bfloat16 [64, 2048, 1408], P('ctx', None, 'sub'), may hold values from -0.125 to 0.125
- w_down: bfloat16 [64, 1408, 2048], P('ctx', 'sub'), may hold values from -0.15625 to 0.15625
Outputs:
- layer_out: bfloat16 [64, 2048], P(('grp', 'ctx'), 'sub'), parts along dimension 0
There are 2 independent parts, one for each index of `grp`. A program takes and returns all parts, laid end to end along the dimension named above; an argument that names none is the same for every part. Nothing has to cross between parts.
Inputs may be any that keep to these rules, and one draw needn't show every extreme that they name: `route_ids`: each row names 6 different experts. Among the 8 rows of one ctx index no expert is named more than 2 times, and in every draw some expert is named exactly 2 times by the rows of some ctx index. cache_len[c] positions at the start of shard c are live; at least one shard is full.
All inputs are finite; a program needn't handle non-finite values.
Results may differ from a plain program's by a relative error of at most 0.015.
Values may be sent and summed in bfloat16 or wider, within the bound.
A program may use at most 128 MiB of HBM per device.

v0:
```python
import jax
import jax.numpy as jnp
from jax import lax
from jax.sharding import PartitionSpec as P

D = 2048
NOPE = 128
ROPE = 64
VDIM = 128
LATENT = 512
TOP = 6
CAP = 2


epsilon = 1e-06


def local_attention(absorbed, cache_rows, length, up_value):
    scores = jnp.einsum("qhc,kc->qhk", absorbed, cache_rows, preferred_element_type=jnp.float32) * (
        NOPE + ROPE
    ) ** (-0.5)
    live_mask = lax.broadcasted_iota(jnp.int32, (cache_rows.shape[0],), 0) < length
    scores = jnp.where(live_mask[None, None, :], scores, -jnp.inf)
    highest = jnp.max(scores, axis=2)
    weights = jnp.exp(scores - highest[:, :, None]).astype(jnp.bfloat16)
    totals = jnp.sum(weights, axis=2, dtype=jnp.float32)
    latent_out = jnp.einsum(
        "qhk,kl->qhl", weights, cache_rows[:, :LATENT], preferred_element_type=jnp.float32
    ).astype(jnp.bfloat16)
    head_out = jnp.einsum("qhl,hvl->qhv", latent_out, up_value, preferred_element_type=jnp.float32)
    return (highest, totals, head_out)


def body(
    queries,
    latent_cache,
    cache_len,
    kv_up,
    o_weight,
    residual,
    norm_gain,
    route_ids,
    route_weights,
    w_gate,
    w_up,
    w_down,
):
    ctx_count = lax.axis_size("ctx")
    sub_count = lax.axis_size("sub")
    heads_dev = kv_up.shape[0]
    token_count = queries.shape[0]
    up_full = lax.all_gather(kv_up, "ctx", axis=2, tiled=True)
    up_key = up_full[:, :NOPE, :]
    up_value = up_full[:, NOPE:, :]
    own_rows = queries.reshape(token_count, heads_dev, NOPE + ROPE)
    query_latent = jnp.einsum(
        "qhn,hnl->qhl", own_rows[:, :, :NOPE], up_key, preferred_element_type=jnp.float32
    ).astype(jnp.bfloat16)
    mine = jnp.concatenate([query_latent, own_rows[:, :, NOPE:]], axis=2).reshape(
        token_count, heads_dev * (LATENT + ROPE)
    )
    absorbed = lax.all_gather(mine, "ctx", axis=0, tiled=True).reshape(-1, heads_dev, LATENT + ROPE)
    highest, totals, head_out = local_attention(absorbed, latent_cache, cache_len[0], up_value)
    all_rows = absorbed.shape[0]
    got_out, got_high, got_total = (
        lax.all_to_all(
            head_out.reshape(all_rows, heads_dev * VDIM),
            "ctx",
            split_axis=0,
            concat_axis=0,
            tiled=True,
        ),
        lax.all_to_all(highest, "ctx", split_axis=0, concat_axis=0, tiled=True),
        lax.all_to_all(totals, "ctx", split_axis=0, concat_axis=0, tiled=True),
    )
    got_out = got_out.reshape(ctx_count, token_count, heads_dev, VDIM)
    got_high = got_high.reshape(ctx_count, token_count, heads_dev)
    got_total = got_total.reshape(ctx_count, token_count, heads_dev)
    overall = jnp.max(got_high, axis=0)
    factor = jnp.exp(got_high - overall[None])
    numerator = jnp.sum(got_out * factor[:, :, :, None], axis=0)
    denominator = jnp.sum(got_total * factor, axis=0)
    attention = (
        (numerator / denominator[:, :, None])
        .astype(jnp.bfloat16)
        .reshape(token_count, heads_dev * VDIM)
    )
    projected = jnp.dot(
        attention,
        lax.all_gather(o_weight, "ctx", axis=1, tiled=True),
        preferred_element_type=jnp.float32,
    )
    quarter = D // sub_count
    offset_cols = lax.axis_index("sub") * quarter
    hidden = residual.astype(jnp.float32) + lax.psum(projected.astype(jnp.bfloat16), "sub").astype(
        jnp.float32
    )
    inverse_rms = lax.rsqrt(jnp.mean(hidden * hidden, axis=1) + epsilon)
    normed = (hidden * inverse_rms[:, None] * norm_gain.astype(jnp.float32)).astype(jnp.bfloat16)
    hidden_part = lax.dynamic_slice_in_dim(hidden, offset_cols, quarter, 1)
    experts_dev = w_gate.shape[0]
    expert_total = experts_dev * ctx_count
    pair_count = token_count * TOP
    expert_ids = route_ids.reshape(pair_count)
    onehot = (expert_ids[:, None] == lax.broadcasted_iota(jnp.int32, (1, expert_total), 1)).astype(
        jnp.int32
    )
    earlier = jnp.cumsum(onehot, axis=0) - onehot
    slot_ids = jnp.sum(earlier * onehot, axis=1)
    targets = (expert_ids * CAP + slot_ids).reshape(token_count, TOP)
    matches = targets[:, :, None] == lax.broadcasted_iota(jnp.int32, (1, 1, expert_total * CAP), 2)
    select = jnp.sum(matches.astype(jnp.int32), axis=1).astype(jnp.bfloat16)
    outgoing = jnp.einsum("tj,td->jd", select, normed, preferred_element_type=jnp.float32).astype(
        jnp.bfloat16
    )
    outgoing = outgoing.reshape(ctx_count, experts_dev, CAP, D)
    received = lax.all_to_all(outgoing, "ctx", split_axis=0, concat_axis=0, tiled=True)
    gate_act = jnp.einsum("sekd,edf->sekf", received, w_gate, preferred_element_type=jnp.float32)
    up_act = jnp.einsum("sekd,edf->sekf", received, w_up, preferred_element_type=jnp.float32)
    gated_rows = (jax.nn.silu(gate_act) * up_act).astype(jnp.bfloat16)
    partial_out = jnp.einsum(
        "sekf,efd->sekd", gated_rows, w_down, preferred_element_type=jnp.float32
    )
    summed = lax.psum_scatter(
        partial_out.astype(jnp.bfloat16), "sub", scatter_dimension=3, tiled=True
    )
    back_rows = lax.all_to_all(summed, "ctx", split_axis=0, concat_axis=0, tiled=True)
    back_rows = back_rows.reshape(expert_total * CAP, quarter)
    mixing = jnp.sum(jnp.where(matches, route_weights[:, :, None], 0.0), axis=1)
    routed = jnp.dot(mixing, back_rows.astype(jnp.float32), precision=lax.Precision.HIGHEST)
    return (hidden_part + routed).astype(jnp.bfloat16)


def solution(mesh):
    in_specs = (
        P(("grp", "ctx"), "sub"),
        P(("grp", "ctx"), None),
        P(("grp", "ctx")),
        P(("grp", "sub"), None, "ctx"),
        P("sub", "ctx"),
        P(("grp", "ctx"), None),
        P(),
        P(("grp", "ctx"), None),
        P(("grp", "ctx"), None),
        P("ctx", None, "sub"),
        P("ctx", None, "sub"),
        P("ctx", "sub", None),
    )
    out_specs = P(("grp", "ctx"), "sub")
    return jax.shard_map(body, mesh=mesh, in_specs=in_specs, out_specs=out_specs, check_vma=False)
```

profile of v0, /device:TPU:0, one launch (start us, length us, event | category | flops | bytes accessed | tf_op | source)
XLA Modules:
  0.0 276.9 jit_solution(12758054297995434755)
XLA Ops:
  12.2 29.3 %all-gather.3.cloned.1.call-done = bf16[4,256,512]{2,1,0:T(8,128)(2,1)} async-done(((bf16[4,256,128]{2,1,0:T(8,128)(2,1)}), bf16[4,256,512]{2,1,0:T(8,128)(2,1)}) %all-gather.3.cloned.1.call-update) | async-done | bytes 1048592 | tf_op jit(solution)/shard_map/all_gather | solution.py:52
  41.6 1.2 fusion.15
  42.9 14.3 %all_gather.10 = bf16[32,2304]{1,0:T(8,128)(2,1)S(1)} all-gather(bf16[8,2304]{1,0:T(8,128)(2,1)S(1)} %reshape.63), channel_id=1, replica_groups=mesh['grp'=2,'ctx'=4,'sub'=4] {'ctx'}, dimensions={0}, use_global_device_ids=true | all-gather | bytes 184320 | tf_op jit(solution)/shard_map/all_gather | solution.py:62
  57.5 1.3 fusion.41
  59.5 4.1 %all-to-all-start.1 = ((f32[4,8,4]{1,2,0:T(4,128)}), f32[4,8,4]{1,2,0:T(4,128)S(1)}, u32[]{:S(2)}, u32[]{:S(2)}) async-start(f32[4,8,4]{1,2,0:T(4,128)} %copy.54), calls=%async_computation.1 | async-start | bytes 16384 | tf_op jit(solution)/shard_map/all_to_all | solution.py:73
  64.5 5.1 %all-to-all-done.1 = f32[4,8,4]{1,2,0:T(4,128)S(1)} async-done(((f32[4,8,4]{1,2,0:T(4,128)}), f32[4,8,4]{1,2,0:T(4,128)S(1)}, u32[]{:S(2)}, u32[]{:S(2)}) %all-to-all-start.1) | async-done | bytes 544 | tf_op jit(solution)/shard_map/all_to_all | solution.py:73
  69.6 3.2 %all-to-all-start.2 = ((f32[4,8,4]{1,2,0:T(4,128)}), f32[4,8,4]{1,2,0:T(4,128)S(1)}, u32[]{:S(2)}, u32[]{:S(2)}) async-start(f32[4,8,4]{1,2,0:T(4,128)} %copy.55), calls=%async_computation.2 | async-start | bytes 16384 | tf_op jit(solution)/shard_map/all_to_all | solution.py:74
  72.8 1.6 fusion.14
  75.2 3.3 %all-to-all-done.2 = f32[4,8,4]{1,2,0:T(4,128)S(1)} async-done(((f32[4,8,4]{1,2,0:T(4,128)}), f32[4,8,4]{1,2,0:T(4,128)S(1)}, u32[]{:S(2)}, u32[]{:S(2)}) %all-to-all-start.2) | async-done | bytes 544 | tf_op jit(solution)/shard_map/all_to_all | solution.py:74
  78.5 3.3 %all-to-all-start = ((f32[4,8,512]{2,1,0:T(8,128)}), f32[4,8,512]{2,1,0:T(8,128)S(1)}, u32[]{:S(2)}, u32[]{:S(2)}) async-start(f32[4,8,512]{2,1,0:T(8,128)} %all_to_all.24), calls=%async_computation | async-start | bytes 131072 | tf_op jit(solution)/shard_map/all_to_all | solution.py:66
  81.9 6.8 %all-to-all-done = f32[4,8,512]{2,1,0:T(8,128)S(1)} async-done(((f32[4,8,512]{2,1,0:T(8,128)}), f32[4,8,512]{2,1,0:T(8,128)S(1)}, u32[]{:S(2)}, u32[]{:S(2)}) %all-to-all-start) | async-done | bytes 65568 | tf_op jit(solution)/shard_map/all_to_all | solution.py:66
  89.5 2.0 convolution_convert_fusion.1
  91.5 11.2 %psum.7 = bf16[8,2048]{1,0:T(8,128)(2,1)S(1)} all-reduce(bf16[8,2048]{1,0:T(8,128)(2,1)S(1)} %convolution_convert_fusion.1), channel_id=1, replica_groups=mesh['grp'=2,'ctx'=4,'sub'=4] {'sub'}, use_global_device_ids=true, to_apply=%region_5.6 | all-reduce | flops 16384 | bytes 65536 | tf_op jit(solution)/shard_map/psum | solution.py:95
  105.0 16.5 %all_to_all.37 = bf16[4,16,2,2048]{3,2,1,0:T(2,128)(2,1)S(1)} all-to-all(bf16[4,16,2,2048]{3,2,1,0:T(2,128)(2,1)S(1)} %reshape.65), channel_id=1, replica_groups=mesh['grp'=2,'ctx'=4,'sub'=4] {'ctx'}, dimensions={0} | all-to-all | bytes 1048576 | tf_op jit(solution)/shard_map/all_to_all | solution.py:117
  121.5 10.9 %fusion.2 = f32[16,4,2,352]{3,2,1,0:T(2,128)S(1)} fusion(bf16[16,2048,352]{1,2,0:T(8,128)(2,1)} %param.22, bf16[4,16,2,2048]{3,2,1,0:T(2,128)(2,1)S(1)} %all_to_all.37), kind=kOutput, calls=%fused_computation.2 | convolution fusion | flops 184549376 | bytes 23773184 | tf_op jit(solution)/shard_map/sekd,edf->sekf/dot_general | solution.py:119
  132.4 10.9 %fusion.4 = f32[16,4,2,352]{3,2,1,0:T(2,128)S(1)} fusion(bf16[16,2048,352]{1,2,0:T(8,128)(2,1)} %param.21, bf16[4,16,2,2048]{3,2,1,0:T(2,128)(2,1)S(1)} %all_to_all.37), kind=kOutput, calls=%fused_computation.4 | convolution fusion | flops 184549376 | bytes 23773184 | tf_op jit(solution)/shard_map/sekd,edf->sekf/dot_general | solution.py:118
  143.4 10.8 %fusion.9 = bf16[4,16,2,2048]{3,0,2,1:T(4,128)(2,1)S(1)} fusion(bf16[16,352,2048]{2,1,0:T(8,128)(2,1)} %param.23, bf16[4,16,2,352]{3,1,2,0:T(8,128)(2,1)S(1)} %fusion.26), kind=kOutput, calls=%fused_computation.8 | convolution fusion | flops 184811520 | bytes 23683072 | tf_op jit(solution)/shard_map/sekf,efd->sekd/dot_general | solution.py:121
  154.2 30.6 %copy.67 = bf16[4,16,2,2048]{0,2,1,3:T(2,128)(2,1)} copy(bf16[4,16,2,2048]{3,0,2,1:T(4,128)(2,1)S(1)} %fusion.9) | data formatting | bytes 1048576
  184.8 31.8 %reshape.72 = bf16[2048,128]{1,0:T(8,128)(2,1)} reshape(bf16[2048,16,2,4]{3,2,1,0:T(2,128)(2,1)} %bitcast.73) | data formatting | bytes 1048576
  216.6 20.8 %reduce-scatter.4.cloned.1.call-done = bf16[512,128]{1,0:T(8,128)(2,1)} async-done(((bf16[2048,128]{1,0:T(8,128)(2,1)}), bf16[512,128]{1,0:T(8,128)(2,1)}) %reduce-scatter.4.cloned.1.call-update) | async-done | bytes 131088
  237.4 10.7 %reshape.73 = bf16[512,16,2,4]{3,2,1,0:T(2,128)(2,1)} reshape(bf16[512,128]{1,0:T(8,128)(2,1)} %reduce-scatter.4.cloned.1.call-done) | data formatting | bytes 262144
  248.2 10.7 %copy.63 = bf16[4,16,2,512]{3,2,1,0:T(2,128)(2,1)} copy(bf16[4,16,2,512]{0,2,1,3:T(2,128)(2,1)} %bitcast.74) | data formatting | bytes 262144 | tf_op jit(solution)/shard_map/reduce_scatter | solution.py:124
  258.8 4.6 %all-to-all-start.4 = ((bf16[4,16,2,512]{3,2,1,0:T(2,128)(2,1)}), bf16[4,16,2,512]{3,2,1,0:T(2,128)(2,1)S(1)}, u32[]{:S(2)}, u32[]{:S(2)}) async-start(bf16[4,16,2,512]{3,2,1,0:T(2,128)(2,1)} %copy.63), calls=%async_computation.4 | async-start | bytes 262144 | tf_op jit(solution)/shard_map/all_to_all | solution.py:127
  263.6 5.9 %all-to-all-done.4 = bf16[4,16,2,512]{3,2,1,0:T(2,128)(2,1)S(1)} async-done(((bf16[4,16,2,512]{3,2,1,0:T(2,128)(2,1)}), bf16[4,16,2,512]{3,2,1,0:T(2,128)(2,1)S(1)}, u32[]{:S(2)}, u32[]{:S(2)}) %all-to-all-start.4) | async-done | bytes 131104 | tf_op jit(solution)/shard_map/all_to_all | solution.py:127
  (46 shorter events, 11.9 us)
Async XLA Ops:
  6.5 35.0 %all-gather.3.cloned.1.call-start = ((), (), s32[]{:S(2)}) async-start(), calls=%async_computation.6 | async-start | bytes 1310720 | tf_op jit(solution)/shard_map/all_gather | solution.py:52
  7.3 82.2 %all-gather.5.cloned.1.call-start = ((), (), s32[]{:S(2)}) async-start(), calls=%async_computation.7 | async-start | bytes 2621440 | tf_op jit(solution)/shard_map/all_gather | solution.py:90
  59.5 10.1 %all-to-all-start.1 = ((f32[4,8,4]{1,2,0:T(4,128)}), f32[4,8,4]{1,2,0:T(4,128)S(1)}, u32[]{:S(2)}, u32[]{:S(2)}) async-start(f32[4,8,4]{1,2,0:T(4,128)} %copy.54), calls=%async_computation.1 | async-start | bytes 16384 | tf_op jit(solution)/shard_map/all_to_all | solution.py:73
  69.6 8.9 %all-to-all-start.2 = ((f32[4,8,4]{1,2,0:T(4,128)}), f32[4,8,4]{1,2,0:T(4,128)S(1)}, u32[]{:S(2)}, u32[]{:S(2)}) async-start(f32[4,8,4]{1,2,0:T(4,128)} %copy.55), calls=%async_computation.2 | async-start | bytes 16384 | tf_op jit(solution)/shard_map/all_to_all | solution.py:74
  78.5 10.2 %all-to-all-start = ((f32[4,8,512]{2,1,0:T(8,128)}), f32[4,8,512]{2,1,0:T(8,128)S(1)}, u32[]{:S(2)}, u32[]{:S(2)}) async-start(f32[4,8,512]{2,1,0:T(8,128)} %all_to_all.24), calls=%async_computation | async-start | bytes 131072 | tf_op jit(solution)/shard_map/all_to_all | solution.py:66
  81.8 155.6 %reduce-scatter.4.cloned.1.call-start = ((), (), s32[]{:S(2)}) async-start(), calls=%async_computation.8 | async-start | bytes 655360
  154.2 109.2 %copy-start = (f32[8,6]{1,0:T(8,128)S(1)}, f32[8,6]{1,0:T(8,128)}, u32[]{:S(2)}) copy-start(f32[8,6]{1,0:T(8,128)} %param.20) | copy-start | bytes 580
  258.8 10.7 %all-to-all-start.4 = ((bf16[4,16,2,512]{3,2,1,0:T(2,128)(2,1)}), bf16[4,16,2,512]{3,2,1,0:T(2,128)(2,1)S(1)}, u32[]{:S(2)}, u32[]{:S(2)}) async-start(bf16[4,16,2,512]{3,2,1,0:T(2,128)(2,1)} %copy.63), calls=%async_computation.4 | async-start | bytes 262144 | tf_op jit(solution)/shard_map/all_to_all | solution.py:127
Sparse Core Ops, SparseCore 0:
  8.9 32.6 all-gather.2
  43.1 46.2 all-gather.4
  216.7 20.6 reduce-scatter.3
where the time goes:
time: 278 us; the launch traced here: 277 us
  local copies, waits for them, and re-layouts  88.4 us (32%)
  waiting for transfers between devices  73.4 us (26%)
  blocking collectives  42 us (15%)
  matrix products  40.6 us (15%)
  starting transfers between devices  15.3 us (6%)
  between operations  14 us (5%)
  other arithmetic  3.18 us (1%)
    unnamed x7, local copies, waits for them, and re-layouts  73.2 us
    all_gather x1, waiting for transfers between devices, body(): up_full = lax.all_gather(kv_up, 'ctx', axis=2, tiled=True)  29.3 us
    unnamed x4, waiting for transfers between devices  22.3 us
    all_to_all x1, blocking collectives, body(): lax.all_to_all(outgoing, 'ctx', split_axis=0, concat_axis=0, tiled=True)  16.5 us
    all_gather x1, blocking collectives, body(): lax.all_gather(mine, 'ctx', axis=0, tiled=True)  14.3 us
    psum x1, blocking collectives, body(): lax.psum(projected.astype(jnp.bfloat16), 'sub').astype(jnp.float32)  11.2 us
    dot_general x1, matrix products, body(): jnp.einsum('sekd,edf->sekf', received, w_gate, preferred_element_type=jnp...  10.9 us
    dot_general x1, matrix products, body(): jnp.einsum('sekd,edf->sekf', received, w_up, preferred_element_type=jnp.f...  10.9 us
  transfers between devices with their start and end apart: 7, of which 7 were waited for; matrix products, arithmetic and copies ran while one was open for 4% of the time, Pallas kernels for 0%

commit v1 on v0

--- a/solution.py
+++ b/solution.py
@@ -1,6 +1,10 @@
+import functools
+
 import jax
 import jax.numpy as jnp
 from jax import lax
+from jax.experimental import pallas as pl
+from jax.experimental.pallas import tpu as pltpu
 from jax.sharding import PartitionSpec as P
 
 D = 2048
@@ -131,6 +135,343 @@
     return (hidden_part + routed).astype(jnp.bfloat16)
 
 
+LANES = 128
+SLOTS = 12
+MESH = pl.DeviceIdType.MESH
+F32 = jnp.float32
+BF16 = jnp.bfloat16
+
+
+def fused_kernel(
+    dims,
+    pack_ref,
+    live_ref,
+    cache_ref,
+    kv_ref,
+    o_ref,
+    gain_ref,
+    gate_hbm,
+    up_hbm,
+    down_hbm,
+    out_ref,
+    pack_all,
+    ql_send,
+    ql_all,
+    lat_send,
+    lat_all,
+    stat_send,
+    stat_all,
+    att_send,
+    att_all,
+    proj_send,
+    proj_all,
+    hid_send,
+    hid_all,
+    normed,
+    total,
+    fin_send,
+    fin_all,
+    gate_buf,
+    up_buf,
+    down_buf,
+    ctx_send,
+    ctx_recv,
+    sub_send,
+    sub_recv,
+    fin_ssem,
+    fin_rsem,
+    w_sem,
+):
+    ctx, sub, tok, heads, experts, slots = dims
+    me_c = lax.axis_index("ctx")
+    me_s = lax.axis_index("sub")
+    span = ctx * tok
+    rows = heads * span
+    quarter = o_ref.shape[1]
+
+    def weight_copies(e, slot):
+        return (
+            pltpu.make_async_copy(gate_hbm.at[e], gate_buf.at[slot], w_sem.at[slot, 0]),
+            pltpu.make_async_copy(up_hbm.at[e], up_buf.at[slot], w_sem.at[slot, 1]),
+            pltpu.make_async_copy(down_hbm.at[e], down_buf.at[slot], w_sem.at[slot, 2]),
+        )
+
+    def prefetch(e, carry):
+        for copy in weight_copies(e, e):
+            copy.start()
+        return carry
+
+    lax.fori_loop(0, slots, prefetch, 0)
+
+    barrier = pltpu.get_barrier_semaphore()
+    for dc in range(ctx):
+        for ds in range(sub):
+            if dc or ds:
+                pl.semaphore_signal(
+                    barrier,
+                    inc=1,
+                    device_id={"ctx": lax.rem(me_c + dc, ctx), "sub": lax.rem(me_s + ds, sub)},
+                    device_id_type=MESH,
+                )
+    pl.semaphore_wait(barrier, ctx * sub - 1)
+
+    def ctx_copy(phase, source_of, target, d):
+        peer = lax.rem(me_c + d, ctx)
+        return pltpu.make_async_remote_copy(
+            src_ref=source_of(peer),
+            dst_ref=target.at[me_c],
+            send_sem=ctx_send.at[phase, d],
+            recv_sem=ctx_recv.at[phase, d],
+            device_id={"ctx": peer},
+            device_id_type=MESH,
+        )
+
+    def ctx_start(phase, source_of, target):
+        copies = [ctx_copy(phase, source_of, target, d) for d in range(1, ctx)]
+        for copy in copies:
+            copy.start()
+        return copies
+
+    def finish(copies):
+        for copy in copies:
+            copy.wait()
+
+    copies = ctx_start(0, lambda peer: pack_ref.at[peer], pack_all)
+    pack_all[me_c] = pack_ref[me_c]
+    finish(copies)
+
+    for h in range(heads):
+        nope = pack_all[:, :, h * 2 * LANES : h * 2 * LANES + NOPE].reshape(span, NOPE).astype(BF16)
+        part = jnp.dot(nope, kv_ref[h, :NOPE, :], preferred_element_type=F32).astype(BF16)
+        ql_send[h * span : (h + 1) * span, :] = part
+    copies = ctx_start(1, lambda peer: ql_send, ql_all)
+    ql_all[me_c] = ql_send[...]
+    rope = jnp.concatenate(
+        [
+            pack_all[:, :, (2 * h + 1) * LANES : (2 * h + 1) * LANES + ROPE].reshape(span, ROPE)
+            for h in range(heads)
+        ],
+        axis=0,
+    ).astype(BF16)
+    nt = (((1,), (1,)), ((), ()))
+    rope_scores = lax.dot_general(rope, cache_ref[:, LATENT:], nt, preferred_element_type=F32)
+    finish(copies)
+    lat_q = jnp.concatenate([ql_all[c] for c in range(ctx)], axis=1)
+    scores = lax.dot_general(lat_q, cache_ref[:, :LATENT], nt, preferred_element_type=F32)
+    scores = (scores + rope_scores) * (NOPE + ROPE) ** (-0.5)
+    scores = jnp.where(live_ref[...] > 0.0, scores, -jnp.inf)
+    highest = jnp.max(scores, axis=1, keepdims=True)
+    weights = jnp.exp(scores - highest).astype(BF16)
+    totals = jnp.sum(weights.astype(F32), axis=1, keepdims=True)
+    lane = lax.broadcasted_iota(jnp.int32, (rows, LANES), 1)
+    stats = jnp.where(lane < 64, highest, totals).T
+    stat_send[0:8, :] = stats[0:8, :]
+    stat_send[8:16, :] = stats[64:72, :]
+    copies = ctx_start(3, lambda peer: stat_send, stat_all)
+    stat_all[me_c] = stat_send[...]
+    latent = jnp.dot(weights, cache_ref[:, :LATENT], preferred_element_type=F32).astype(BF16)
+    for c in range(ctx):
+        lat_send[c] = latent[:, c * LANES : (c + 1) * LANES]
+    copies += ctx_start(2, lambda peer: lat_send.at[peer], lat_all)
+    lat_all[me_c] = lat_send[me_c]
+    finish(copies)
+
+    highs = [stat_all[c, 0:1, :] for c in range(ctx)]
+    overall = functools.reduce(jnp.maximum, highs)
+    factors = [jnp.exp(high - overall) for high in highs]
+    denominator = sum(f * stat_all[c, 8:9, :] for c, f in enumerate(factors))
+    merged = jnp.zeros((rows, LANES), F32)
+    for c in range(ctx):
+        scale = jnp.broadcast_to(factors[c] / denominator, (LANES, rows)).T
+        merged += lat_all[c].astype(F32) * scale
+    merged = merged.astype(BF16)
+    for h in range(heads):
+        part = lax.dot_general(
+            merged[h * span : (h + 1) * span, :],
+            kv_ref[h, NOPE:, :],
+            nt,
+            preferred_element_type=F32,
+        )
+        att_send[:, h * VDIM : (h + 1) * VDIM] = part.astype(BF16)
+    copies = ctx_start(4, lambda peer: att_send, att_all)
+    att_all[me_c] = att_send[...]
+    finish(copies)
+    attention = sum(att_all[c].astype(F32) for c in range(ctx)).astype(BF16)
+    proj_send[...] = jnp.dot(attention, o_ref[...], preferred_element_type=F32).astype(BF16)
+    copies = [
+        pltpu.make_async_remote_copy(
+            src_ref=proj_send,
+            dst_ref=proj_all.at[me_s],
+            send_sem=sub_send.at[d],
+            recv_sem=sub_recv.at[d],
+            device_id={"sub": lax.rem(me_s + d, sub)},
+            device_id_type=MESH,
+        )
+        for d in range(1, sub)
+    ]
+    for copy in copies:
+        copy.start()
+    proj_all[me_s] = proj_send[...]
+    residual = pack_all[:, :, heads * 2 * LANES : heads * 2 * LANES + quarter].reshape(span, quarter)
+    finish(copies)
+    hid_send[...] = residual + sum(proj_all[s].astype(F32) for s in range(sub))
+    copies = ctx_start(5, lambda peer: hid_send, hid_all)
+    hid_all[me_c] = hid_send[...]
+    finish(copies)
+
+    squares = sum(
+        jnp.sum(hid_all[c] * hid_all[c], axis=1, keepdims=True) for c in range(ctx)
+    )
+    inverse_rms = lax.rsqrt(squares / (ctx * quarter) + epsilon)
+    for c in range(ctx):
+        cols = slice(c * quarter, (c + 1) * quarter)
+        normed[:, cols] = (hid_all[c] * inverse_rms * gain_ref[:, cols]).astype(BF16)
+
+    total[...] = jnp.zeros_like(total)
+    comb = pack_all[:, :, heads * 2 * LANES + quarter :].reshape(span, LANES)
+    comb_lane = lax.broadcasted_iota(jnp.int32, (span, LANES), 1)
+
+    def expert(e, carry):
+        slot = lax.rem(e, slots)
+        gate_copy, up_copy, down_copy = weight_copies(e, slot)
+        gate_copy.wait()
+        gate_act = jnp.dot(normed[...], gate_buf[slot], preferred_element_type=F32)
+        up_copy.wait()
+        up_act = jnp.dot(normed[...], up_buf[slot], preferred_element_type=F32)
+        gated = (gate_act / (1.0 + jnp.exp(-gate_act)) * up_act).astype(BF16)
+        down_copy.wait()
+        mix = jnp.sum(jnp.where(comb_lane == e, comb, 0.0), axis=1, keepdims=True)
+        total[...] += mix * jnp.dot(gated, down_buf[slot], preferred_element_type=F32)
+        return carry
+
+    def expert_and_refill(e, carry):
+        expert(e, carry)
+        for copy in weight_copies(e + slots, lax.rem(e, slots)):
+            copy.start()
+        return carry
+
+    lax.fori_loop(0, experts - slots, expert_and_refill, 0)
+    lax.fori_loop(experts - slots, experts, expert, 0)
+
+    for c in range(ctx):
+        for s in range(sub):
+            fin_send[c * sub + s] = total[
+                c * tok : (c + 1) * tok, s * quarter : (s + 1) * quarter
+            ].astype(BF16)
+    copies = []
+    for dc in range(ctx):
+        for ds in range(sub):
+            if dc or ds:
+                peer_c, peer_s = lax.rem(me_c + dc, ctx), lax.rem(me_s + ds, sub)
+                copies.append(
+                    pltpu.make_async_remote_copy(
+                        src_ref=fin_send.at[peer_c * sub + peer_s],
+                        dst_ref=fin_all.at[me_c * sub + me_s],
+                        send_sem=fin_ssem.at[dc * sub + ds],
+                        recv_sem=fin_rsem.at[dc * sub + ds],
+                        device_id={"ctx": peer_c, "sub": peer_s},
+                        device_id_type=MESH,
+                    )
+                )
+                copies[-1].start()
+    me = me_c * sub + me_s
+    fin_all[me] = fin_send[me]
+    hidden = hid_all[me_s, pl.ds(pl.multiple_of(me_c * tok, tok), tok), :]
+    finish(copies)
+    routed = sum(fin_all[i].astype(F32) for i in range(ctx * sub))
+    out_ref[...] = (hidden + routed).astype(out_ref.dtype)
+
+
+def fused_body(
+    queries,
+    latent_cache,
+    cache_len,
+    kv_up,
+    o_weight,
+    residual,
+    norm_gain,
+    route_ids,
+    route_weights,
+    w_gate,
+    w_up,
+    w_down,
+):
+    ctx, sub = lax.axis_size("ctx"), lax.axis_size("sub")
+    heads, tok, experts = kv_up.shape[0], queries.shape[0], w_gate.shape[0]
+    span, rows, quarter = ctx * tok, heads * ctx * tok, o_weight.shape[1]
+    width = residual.shape[1]
+    slots = min(SLOTS, experts)
+    q = queries.astype(F32).reshape(tok, heads, NOPE + ROPE)
+    q = jnp.pad(q, ((0, 0), (0, 0), (0, 2 * LANES - NOPE - ROPE))).reshape(1, tok, heads * 2 * LANES)
+    res = residual.astype(F32).reshape(tok, ctx, quarter).transpose(1, 0, 2)
+    names = (
+        lax.broadcasted_iota(jnp.int32, (ctx, 1, 1, LANES), 0) * experts
+        + lax.broadcasted_iota(jnp.int32, (ctx, 1, 1, LANES), 3)
+    )
+    inside = lax.broadcasted_iota(jnp.int32, (ctx, 1, 1, LANES), 3) < experts
+    hit = (route_ids[None, :, :, None] == names) & inside
+    comb = jnp.sum(jnp.where(hit, route_weights[None, :, :, None], 0.0), axis=2)
+    pack = jnp.concatenate([jnp.broadcast_to(q, (ctx,) + q.shape[1:]), res, comb], axis=2)
+    count = latent_cache.shape[0]
+    live = (lax.broadcasted_iota(jnp.int32, (1, count), 1) < cache_len[0]).astype(F32)
+    gain = norm_gain.astype(F32).reshape(1, width)
+    vmem = pl.BlockSpec(memory_space=pltpu.VMEM)
+    hbm = pl.BlockSpec(memory_space=pl.ANY)
+    dma = pltpu.SemaphoreType.DMA
+    return pl.pallas_call(
+        functools.partial(fused_kernel, (ctx, sub, tok, heads, experts, slots)),
+        out_shape=jax.ShapeDtypeStruct((tok, width // sub), BF16),
+        in_specs=[vmem] * 6 + [hbm] * 3,
+        out_specs=vmem,
+        scratch_shapes=[
+            pltpu.VMEM(pack.shape, F32),
+            pltpu.VMEM((rows, LANES), BF16),
+            pltpu.VMEM((ctx, rows, LANES), BF16),
+            pltpu.VMEM((ctx, rows, LANES), BF16),
+            pltpu.VMEM((ctx, rows, LANES), BF16),
+            pltpu.VMEM((16, rows), F32),
+            pltpu.VMEM((ctx, 16, rows), F32),
+            pltpu.VMEM((span, heads * VDIM), BF16),
+            pltpu.VMEM((ctx, span, heads * VDIM), BF16),
+            pltpu.VMEM((span, quarter), BF16),
+            pltpu.VMEM((sub, span, quarter), BF16),
+            pltpu.VMEM((span, quarter), F32),
+            pltpu.VMEM((ctx, span, quarter), F32),
+            pltpu.VMEM((span, width), BF16),
+            pltpu.VMEM((span, width), F32),
+            pltpu.VMEM((ctx * sub, tok, quarter), BF16),
+            pltpu.VMEM((ctx * sub, tok, quarter), BF16),
+            pltpu.VMEM((slots,) + w_gate.shape[1:], BF16),
+            pltpu.VMEM((slots,) + w_up.shape[1:], BF16),
+            pltpu.VMEM((slots,) + w_down.shape[1:], BF16),
+            dma((6, ctx)),
+            dma((6, ctx)),
+            dma((sub,)),
+            dma((sub,)),
+            dma((ctx * sub,)),
+            dma((ctx * sub,)),
+            dma((slots, 3)),
+        ],
+        compiler_params=pltpu.CompilerParams(
+            collective_id=0, has_side_effects=True, vmem_limit_bytes=67043328
+        ),
+    )(pack, live, latent_cache, kv_up, o_weight, gain, w_gate, w_up, w_down)
+
+
+def choose_body(*args):
+    kv_up, o_weight, w_gate = args[3], args[4], args[9]
+    ctx, sub, tok = lax.axis_size("ctx"), lax.axis_size("sub"), args[0].shape[0]
+    fits = (
+        ctx == sub
+        and kv_up.shape[2] == LANES
+        and o_weight.shape[1] % LANES == 0
+        and kv_up.shape[0] * ctx * tok == LANES
+        and w_gate.shape[0] <= LANES
+        and tok % 8 == 0
+    )
+    return fused_body(*args) if fits else body(*args)
+
+
 def solution(mesh):
     in_specs = (
         P(("grp", "ctx"), "sub"),
@@ -147,4 +488,4 @@
         P("ctx", "sub", None),
     )
     out_specs = P(("grp", "ctx"), "sub")
-    return jax.shard_map(body, mesh=mesh, in_specs=in_specs, out_specs=out_specs, check_vma=False)
+    return jax.shard_map(choose_body, mesh=mesh, in_specs=in_specs, out_specs=out_specs, check_vma=False)

time: 278 us -> 136 us (0.49)
  waiting for transfers between devices: 73.4 us -> 0 us
  Pallas kernels: 0 us -> 63.5 us
  blocking collectives: 42 us -> 0 us
  matrix products: 40.6 us -> 0 us
  local copies, waits for them, and re-layouts: 88.4 us -> 66 us
  starting transfers between devices: 15.3 us -> 0 us
  between operations: 14 us -> 0.71 us
    pallas_call x0 -> x1, Pallas kernels: none -> 63.5 us  [fused_body(): pl.pallas_call(functools.partial(fused_kernel, (ctx, sub, tok, heads, exp...]
    dot_general x9 -> x0, matrix products: 40.6 us -> none  [the longest x1 10.9 us: body(): jnp.einsum('sekd,edf->sekf', received, w_gate, preferred_element_type=jnp...]
    all_gather x2 -> x0, waiting for transfers between devices: 30 us -> none  [the longest x1 29.3 us: body(): up_full = lax.all_gather(kv_up, 'ctx', axis=2, tiled=True)]
    unnamed x4 -> x0, waiting for transfers between devices: 22.3 us -> none
    all_to_all x4 -> x0, waiting for transfers between devices: 21.1 us -> none  [the longest x1 6.85 us: body(): lax.all_to_all(head_out.reshape(all_rows, heads_dev * VDIM), 'ctx', split...]
    all_to_all x1 -> x0, blocking collectives: 16.5 us -> none  [body(): lax.all_to_all(outgoing, 'ctx', split_axis=0, concat_axis=0, tiled=True)]
    all_to_all x4 -> x0, starting transfers between devices: 15.2 us -> none  [the longest x1 4.6 us: body(): lax.all_to_all(summed, 'ctx', split_axis=0, concat_axis=0, tiled=True)]
    all_gather x1 -> x0, blocking collectives: 14.3 us -> none  [body(): lax.all_gather(mine, 'ctx', axis=0, tiled=True)]
  transfers between devices with their start and end apart: 7 -> 0, of which waited for: 7 -> 0; matrix products, arithmetic and copies ran while one was open for 4% -> 0% of each run, Pallas kernels for 0% -> 0%
where the time goes in v1:
time: 136 us; the launch traced here: 134 us
  local copies, waits for them, and re-layouts  66 us (49%)
  Pallas kernels  63.5 us (47%)
  other arithmetic  3.49 us (3%)
    unnamed x7, local copies, waits for them, and re-layouts  65.2 us
    pallas_call x1, Pallas kernels, fused_body(): pl.pallas_call(functools.partial(fused_kernel, (ctx, sub, tok, heads, exp...  63.5 us

profile of v1, /device:TPU:0, one launch (start us, length us, event | category | flops | bytes accessed | tf_op | source)
XLA Modules:
  0.0 133.8 jit_solution(16687305582662031861)
XLA Ops:
  0.7 0.5 compare_convert_fusion.live_ref
  1.2 0.1 iota_add_fusion
  1.3 0.8 copy.16
  2.1 0.8 copy.17
  2.8 0.1 select_reduce_fusion
  2.9 1.3 reshape.50
  4.2 0.8 reshape.45
  5.0 0.8 convert_bitcast_fusion
  5.8 0.7 pad_maximum_fusion.pack_ref
  6.5 2.0 %copy.18.cache_ref = bf16[384,576]{1,0:T(8,128)(2,1)} copy(bf16[384,576]{0,1:T(8,128)(2,1)} %param.13) | data formatting | bytes 884736 | tf_op args[1]
  8.5 31.3 %copy.19.gate_hbm = bf16[16,2048,352]{2,1,0:T(8,128)(2,1)} copy(bf16[16,2048,352]{1,2,0:T(8,128)(2,1)} %param.21) | data formatting | bytes 46137344 | tf_op args[9]
  39.8 29.1 %copy.20.up_hbm = bf16[16,2048,352]{2,1,0:T(8,128)(2,1)} copy(bf16[16,2048,352]{1,2,0:T(8,128)(2,1)} %param.22) | data formatting | bytes 46137344 | tf_op args[10]
  68.9 63.5 %shard_map.118 = bf16[8,512]{1,0:T(8,128)(2,1)} custom-call(f32[4,8,1664]{2,1,0:T(8,128)} %pad_maximum_fusion.pack_ref, f32[1,384]{1,0:T(1,128)} %compare_convert_fusion.live_ref, bf16[384,576]{1,0:T(8,128)(2,1)} %copy.18.cache_ref, bf16[4,256,128]{2,1,0:T(8,128)(2,1)} %kv_ref.1, bf16[512,512]{1,0:T(8,128)(2,1)} %o_ref.1, f32[1,2048]{1,0:T(1,128)} %bitcast.12, ...), custom_call_target="tpu_custom_call" | custom-call | tf_op jit(solution)/shard_map/pallas_call | solution.py:421
  132.5 1.3 copy.24
  (5 shorter events, 0.0 us)

commit v2 on v1

--- a/solution.py
+++ b/solution.py
@@ -144,7 +144,10 @@
 
 def fused_kernel(
     dims,
-    pack_ref,
+    q_ref,
+    res_ref,
+    ids_ref,
+    mix_ref,
     live_ref,
     cache_ref,
     kv_ref,
@@ -154,7 +157,10 @@
     up_hbm,
     down_hbm,
     out_ref,
-    pack_all,
+    q_all,
+    res_all,
+    comb_send,
+    comb_all,
     ql_send,
     ql_all,
     lat_send,
@@ -236,28 +242,45 @@
         for copy in copies:
             copy.wait()
 
-    copies = ctx_start(0, lambda peer: pack_ref.at[peer], pack_all)
-    pack_all[me_c] = pack_ref[me_c]
+    def own_columns(peer):
+        return pl.ds(pl.multiple_of(peer * quarter, quarter), quarter)
+
+    copies = ctx_start(0, lambda peer: q_ref, q_all)
+    early = ctx_start(6, lambda peer: res_ref.at[:, own_columns(peer)], res_all)
+    q_all[me_c] = q_ref[...]
+    res_all[me_c] = res_ref[:, own_columns(me_c)]
+    lane = lax.broadcasted_iota(jnp.int32, (tok, LANES), 1)
+    ids, mixes = ids_ref[...], mix_ref[...]
+    for c in range(ctx):
+        comb = jnp.zeros((tok, LANES), F32)
+        for k in range(TOP):
+            hit = (ids[:, k : k + 1] == lane + c * experts) & (lane < experts)
+            comb += jnp.where(hit, mixes[:, k : k + 1], 0.0)
+        comb_send[c] = comb
+    early += ctx_start(7, lambda peer: comb_send.at[peer], comb_all)
+    comb_all[me_c] = comb_send[me_c]
     finish(copies)
 
+    per_head = NOPE + ROPE
+    q_rows = q_all[...].astype(F32).reshape(span, heads * per_head)
+    turned = [
+        q_rows if h == 0 else pltpu.roll(q_rows, (heads - h) * per_head, 1) for h in range(heads)
+    ]
     for h in range(heads):
-        nope = pack_all[:, :, h * 2 * LANES : h * 2 * LANES + NOPE].reshape(span, NOPE).astype(BF16)
+        nope = turned[h][:, :NOPE].astype(BF16)
         part = jnp.dot(nope, kv_ref[h, :NOPE, :], preferred_element_type=F32).astype(BF16)
         ql_send[h * span : (h + 1) * span, :] = part
     copies = ctx_start(1, lambda peer: ql_send, ql_all)
     ql_all[me_c] = ql_send[...]
     rope = jnp.concatenate(
-        [
-            pack_all[:, :, (2 * h + 1) * LANES : (2 * h + 1) * LANES + ROPE].reshape(span, ROPE)
-            for h in range(heads)
-        ],
+        [turned[h][:, NOPE:per_head] for h in range(heads)],
         axis=0,
     ).astype(BF16)
     nt = (((1,), (1,)), ((), ()))
-    rope_scores = lax.dot_general(rope, cache_ref[:, LATENT:], nt, preferred_element_type=F32)
+    rope_scores = jnp.dot(rope, cache_ref[LATENT:, :], preferred_element_type=F32)
     finish(copies)
     lat_q = jnp.concatenate([ql_all[c] for c in range(ctx)], axis=1)
-    scores = lax.dot_general(lat_q, cache_ref[:, :LATENT], nt, preferred_element_type=F32)
+    scores = jnp.dot(lat_q, cache_ref[:LATENT, :], preferred_element_type=F32)
     scores = (scores + rope_scores) * (NOPE + ROPE) ** (-0.5)
     scores = jnp.where(live_ref[...] > 0.0, scores, -jnp.inf)
     highest = jnp.max(scores, axis=1, keepdims=True)
@@ -269,7 +292,9 @@
     stat_send[8:16, :] = stats[64:72, :]
     copies = ctx_start(3, lambda peer: stat_send, stat_all)
     stat_all[me_c] = stat_send[...]
-    latent = jnp.dot(weights, cache_ref[:, :LATENT], preferred_element_type=F32).astype(BF16)
+    latent = lax.dot_general(
+        weights, cache_ref[:LATENT, :], nt, preferred_element_type=F32
+    ).astype(BF16)
     for c in range(ctx):
         lat_send[c] = latent[:, c * LANES : (c + 1) * LANES]
     copies += ctx_start(2, lambda peer: lat_send.at[peer], lat_all)
@@ -312,8 +337,8 @@
     for copy in copies:
         copy.start()
     proj_all[me_s] = proj_send[...]
-    residual = pack_all[:, :, heads * 2 * LANES : heads * 2 * LANES + quarter].reshape(span, quarter)
-    finish(copies)
+    finish(copies + early)
+    residual = res_all[...].astype(F32).reshape(span, quarter)
     hid_send[...] = residual + sum(proj_all[s].astype(F32) for s in range(sub))
     copies = ctx_start(5, lambda peer: hid_send, hid_all)
     hid_all[me_c] = hid_send[...]
@@ -328,16 +353,16 @@
         normed[:, cols] = (hid_all[c] * inverse_rms * gain_ref[:, cols]).astype(BF16)
 
     total[...] = jnp.zeros_like(total)
-    comb = pack_all[:, :, heads * 2 * LANES + quarter :].reshape(span, LANES)
+    comb = comb_all[...].reshape(span, LANES)
     comb_lane = lax.broadcasted_iota(jnp.int32, (span, LANES), 1)
 
     def expert(e, carry):
         slot = lax.rem(e, slots)
         gate_copy, up_copy, down_copy = weight_copies(e, slot)
         gate_copy.wait()
-        gate_act = jnp.dot(normed[...], gate_buf[slot], preferred_element_type=F32)
+        gate_act = lax.dot_general(normed[...], gate_buf[slot], nt, preferred_element_type=F32)
         up_copy.wait()
-        up_act = jnp.dot(normed[...], up_buf[slot], preferred_element_type=F32)
+        up_act = lax.dot_general(normed[...], up_buf[slot], nt, preferred_element_type=F32)
         gated = (gate_act / (1.0 + jnp.exp(-gate_act)) * up_act).astype(BF16)
         down_copy.wait()
         mix = jnp.sum(jnp.where(comb_lane == e, comb, 0.0), axis=1, keepdims=True)
@@ -401,17 +426,7 @@
     span, rows, quarter = ctx * tok, heads * ctx * tok, o_weight.shape[1]
     width = residual.shape[1]
     slots = min(SLOTS, experts)
-    q = queries.astype(F32).reshape(tok, heads, NOPE + ROPE)
-    q = jnp.pad(q, ((0, 0), (0, 0), (0, 2 * LANES - NOPE - ROPE))).reshape(1, tok, heads * 2 * LANES)
-    res = residual.astype(F32).reshape(tok, ctx, quarter).transpose(1, 0, 2)
-    names = (
-        lax.broadcasted_iota(jnp.int32, (ctx, 1, 1, LANES), 0) * experts
-        + lax.broadcasted_iota(jnp.int32, (ctx, 1, 1, LANES), 3)
-    )
-    inside = lax.broadcasted_iota(jnp.int32, (ctx, 1, 1, LANES), 3) < experts
-    hit = (route_ids[None, :, :, None] == names) & inside
-    comb = jnp.sum(jnp.where(hit, route_weights[None, :, :, None], 0.0), axis=2)
-    pack = jnp.concatenate([jnp.broadcast_to(q, (ctx,) + q.shape[1:]), res, comb], axis=2)
+    w_gate, w_up = jnp.swapaxes(w_gate, 1, 2), jnp.swapaxes(w_up, 1, 2)
     count = latent_cache.shape[0]
     live = (lax.broadcasted_iota(jnp.int32, (1, count), 1) < cache_len[0]).astype(F32)
     gain = norm_gain.astype(F32).reshape(1, width)
@@ -421,10 +436,13 @@
     return pl.pallas_call(
         functools.partial(fused_kernel, (ctx, sub, tok, heads, experts, slots)),
         out_shape=jax.ShapeDtypeStruct((tok, width // sub), BF16),
-        in_specs=[vmem] * 6 + [hbm] * 3,
+        in_specs=[vmem] * 9 + [hbm] * 3,
         out_specs=vmem,
         scratch_shapes=[
-            pltpu.VMEM(pack.shape, F32),
+            pltpu.VMEM((ctx,) + queries.shape, BF16),
+            pltpu.VMEM((ctx, tok, quarter), BF16),
+            pltpu.VMEM((ctx, tok, LANES), F32),
+            pltpu.VMEM((ctx, tok, LANES), F32),
             pltpu.VMEM((rows, LANES), BF16),
             pltpu.VMEM((ctx, rows, LANES), BF16),
             pltpu.VMEM((ctx, rows, LANES), BF16),
@@ -444,8 +462,8 @@
             pltpu.VMEM((slots,) + w_gate.shape[1:], BF16),
             pltpu.VMEM((slots,) + w_up.shape[1:], BF16),
             pltpu.VMEM((slots,) + w_down.shape[1:], BF16),
-            dma((6, ctx)),
-            dma((6, ctx)),
+            dma((8, ctx)),
+            dma((8, ctx)),
             dma((sub,)),
             dma((sub,)),
             dma((ctx * sub,)),
@@ -455,7 +473,20 @@
         compiler_params=pltpu.CompilerParams(
             collective_id=0, has_side_effects=True, vmem_limit_bytes=67043328
         ),
-    )(pack, live, latent_cache, kv_up, o_weight, gain, w_gate, w_up, w_down)
+    )(
+        queries,
+        residual,
+        route_ids,
+        route_weights,
+        live,
+        latent_cache.T,
+        kv_up,
+        o_weight,
+        gain,
+        w_gate,
+        w_up,
+        w_down,
+    )
 
 
 def choose_body(*args):

time: 136 us -> 73.7 us (0.54); the launches traced: 134 us -> 73.4 us
  local copies, waits for them, and re-layouts: 66 us -> 1.3 us
  Pallas kernels: 63.5 us -> 69.6 us
  other arithmetic: 3.49 us -> 1.88 us
    unnamed x7 -> x1, local copies, waits for them, and re-layouts: 65.2 us -> 1.3 us
    pallas_call x1, Pallas kernels: 63.5 us -> 69.6 us  [fused_body(): pl.pallas_call(functools.partial(fused_kernel, (ctx, sub, tok, heads, exp...]
where the time goes in v2:
time: 73.7 us; the launch traced here: 73.4 us
  Pallas kernels  69.6 us (94%)
  other arithmetic  1.88 us (3%)
  local copies, waits for them, and re-layouts  1.3 us (2%)
    pallas_call x1, Pallas kernels, fused_body(): pl.pallas_call(functools.partial(fused_kernel, (ctx, sub, tok, heads, exp...  69.6 us

profile of v2, /device:TPU:0, one launch (start us, length us, event | category | flops | bytes accessed | tf_op | source)
XLA Modules:
  0.0 73.4 jit_solution(6907405602433030754)
XLA Ops:
  0.7 0.6 compare_convert_fusion.live_ref
  1.2 1.3 %reshape.19 = f32[2048]{0:T(1024)} convert(bf16[2048]{0:T(1024)(128)(2,1)} %param.18) | non-fusion elementwise | flops 2048 | bytes 12288 | tf_op jit(solution)/shard_map/reshape | solution.py:432
  2.5 69.6 %shard_map.118 = bf16[8,512]{1,0:T(8,128)(2,1)} custom-call(bf16[8,768]{1,0:T(8,128)(2,1)} %q_ref.1, bf16[8,2048]{1,0:T(8,128)(2,1)} %res_ref.1, s32[8,6]{1,0:T(8,128)} %ids_ref.1, f32[8,6]{1,0:T(8,128)} %mix_ref.1, f32[1,384]{1,0:T(1,128)} %compare_convert_fusion.live_ref, bf16[576,384]{1,0:T(8,128)(2,1)} %bitcast.8, bf16[4,256,128]{2,1,0:T(8,128)(2,1)} %kv_ref.1, ...), custom_call_target="tpu_custom_call" | custom-call | tf_op jit(solution)/shard_map/pallas_call | solution.py:436
  72.1 1.3 %copy.15 = bf16[8,512]{1,0:T(8,128)(2,1)} copy(bf16[8,512]{1,0:T(8,128)(2,1)} %shard_map.118) | data formatting | bytes 16384
